TPU v7x, 128 devices: a whole 4x4x4 slice. The times are simulated.
128 devices in a mesh: row: 8 (over z, y_lo), col: 16 (over y_hi, x, core).
Axes of the slice: x: 4, y: 4 (y_hi: 2, y_lo: 2; y = y_hi * 2 + y_lo), z: 4, core: 2. Of those that a mesh axis runs over, the one named last changes fastest.
Arguments:
- blocks: float32 [8, 16, 170, 128, 128], P('row', 'col'), may hold values from -1 to 1
- coords: int32 [8, 16, 2, 170], P('row', 'col'), may hold values from 0 to 31, as said below
- vectors: float32 [2, 32768, 128], P(None, ('row', 'col')), may hold values from -6 to 6
Outputs:
- basis: float32 [2, 32768, 128], P(None, ('row', 'col'))
Inputs may be any that keep to these rules, and one draw needn't show every extreme that they name: Within each tile the 170 listed positions are distinct, and the positions (0, 0) and (31, 15) are always listed; coords[r, c, 0, k] is below 32 and coords[r, c, 1, k] below 16.
All inputs are finite; a program needn't handle non-finite values.
Results may differ from a plain program's by a relative error of at most 0.0003.
Values sent between devices are 32-bit elements; how exact they have to be, the bound alone decides.
A program may use at most 192 MiB of HBM per device.

v0:
```python
import jax
import jax.numpy as jnp
from jax import lax
from jax.sharding import PartitionSpec as P

APPS = 2
exact_mode = lax.Precision.HIGHEST


def tile_products(values, places, col_side, row_side):
    blk_size = values.shape[1]
    listed = values.shape[0]
    row_blocks = row_side.shape[0] // blk_size
    col_blocks = col_side.shape[0] // blk_size
    row_of = places[0]
    col_of = places[1]
    col_pieces = col_side.reshape(col_blocks, blk_size, -1)[col_of]
    direct = jnp.einsum("kab,kbv->kav", values, col_pieces, precision=exact_mode)
    row_pieces = row_side.reshape(row_blocks, blk_size, -1)[row_of]
    flipped = jnp.einsum("kba,kbv->kav", values, row_pieces, precision=exact_mode)
    row_hot = (row_of[None, :] == jnp.arange(row_blocks, dtype=jnp.int32)[:, None]).astype(
        values.dtype
    )
    col_hot = (col_of[None, :] == jnp.arange(col_blocks, dtype=jnp.int32)[:, None]).astype(
        values.dtype
    )
    out_rows = jnp.dot(row_hot, direct.reshape(listed, -1), precision=exact_mode).reshape(
        row_side.shape[0], -1
    )
    out_cols = jnp.dot(col_hot, flipped.reshape(listed, -1), precision=exact_mode).reshape(
        col_side.shape[0], -1
    )
    return (out_rows, out_cols)


def normal_basis(applied, factor):
    return lax.linalg.triangular_solve(
        factor, applied, left_side=False, lower=True, transpose_a=True
    )


def local(blocks, coords, vectors):
    n_rowdev = lax.axis_size("row")
    n_coldev = lax.axis_size("col")
    group_rows = vectors.shape[1]
    total_rows = 2 * group_rows * n_rowdev * n_coldev
    values = blocks.reshape(blocks.shape[2], blocks.shape[3], blocks.shape[4])
    places = coords.reshape(2, coords.shape[3])
    start = (vectors[0], vectors[1])
    current = start
    for app_index in range(APPS):
        col_side = lax.all_gather(current[1], "row", axis=0, tiled=True)
        row_side = lax.all_gather(current[0], "col", axis=0, tiled=True)
        out_rows, out_cols = tile_products(values, places, col_side, row_side)
        new_upper = lax.psum_scatter(out_rows, "col", scatter_dimension=0, tiled=True)
        new_lower = lax.psum_scatter(out_cols, "row", scatter_dimension=0, tiled=True)
        applied = (new_upper, new_lower)
        factor_upper, factor_lower = applied
        partial_gram = jnp.einsum("nv,nw->vw", factor_upper, factor_upper, precision=exact_mode)
        partial_gram = partial_gram + jnp.einsum(
            "nv,nw->vw", factor_lower, factor_lower, precision=exact_mode
        )
        gram_sum = lax.psum(partial_gram, ("row", "col")) / total_rows
        factor = jnp.linalg.cholesky(gram_sum)
        current = (normal_basis(applied[0], factor), normal_basis(applied[1], factor))
    upper, lower = current
    return jnp.stack([upper, lower])


def solution(mesh):
    return jax.shard_map(
        local,
        mesh=mesh,
        in_specs=(
            P("row", "col", None, None, None),
            P("row", "col", None, None),
            P(None, ("row", "col"), None),
        ),
        out_specs=P(None, ("row", "col"), None),
        check_vma=False,
    )
```

profile of v0, /device:TPU:1, one launch (start us, length us, event | category | flops | bytes accessed | tf_op | source)
XLA Modules:
  0.0 845.6 jit_solution(6474394078749091209)
XLA Ops:
  10.6 37.6 %all-gather.11.cloned.1.call-done = f32[1,2048,128]{2,1,0:T(8,128)} async-done(((f32[1,256,128]{2,1,0:T(8,128)}), f32[1,2048,128]{2,1,0:T(8,128)}) %all-gather.11.cloned.1.call-update) | async-done | bytes 1048592 | tf_op jit(solution)/shard_map/all_gather | solution.py:52
  48.2 11.6 %gather_fusion = f32[170,128,128]{2,1,0:T(8,128)} fusion(f32[16,128,128]{2,1,0:T(8,128)} %bitcast.108, s32[1024]{0:T(1024)S(1)} %pad_clamp_fusion.1), kind=kCustom, calls=%fused_computation | custom fusion | bytes 22282920 | tf_op jit(solution)/shard_map/gather | solution.py:17
  59.8 23.3 %fusion.8 = f32[170,128,128]{1,2,0:T(8,128)} fusion(f32[170,128,128]{2,1,0:T(8,128)} %gather_fusion, f32[1,1,170,128,128]{4,3,2,1,0:T(8,128)} %param.6), kind=kOutput, calls=%fused_computation.12 | convolution fusion | flops 4278190080 | bytes 33423360 | tf_op jit(solution)/shard_map/kab,kbv->kav/dot_general | solution.py:18
  83.1 12.3 %copy.12 = f32[170,128,128]{2,1,0:T(8,128)} copy(f32[170,128,128]{1,2,0:T(8,128)} %fusion.8) | data formatting | bytes 22282240 | tf_op jit(solution)/shard_map/kab,kbv->kav/dot_general | solution.py:18
  95.3 10.5 %pad.6 = f32[176,128,128]{2,1,0:T(8,128)} pad(f32[170,128,128]{2,1,0:T(8,128)} %copy.12, f32[]{:T(128)} %constant.31.clone.2), padding=0_6x0_0x0_0 | pad | bytes 22675460
  105.8 18.3 %copy.38 = f32[22,8,128,128]{3,1,2,0:T(8,128)} copy(f32[22,8,128,128]{3,2,1,0:T(8,128)} %bitcast.115) | data formatting | bytes 23068672
  124.1 7.0 fusion.31
  132.8 12.0 %gather_fusion.1 = f32[170,128,128]{2,1,0:T(8,128)} fusion(f32[32,128,128]{2,1,0:T(8,128)} %bitcast.110, s32[1024]{0:T(1024)S(1)} %pad_clamp_fusion), kind=kCustom, calls=%fused_computation.1 | custom fusion | bytes 22282920 | tf_op jit(solution)/shard_map/gather | solution.py:19
  144.8 23.4 %fusion.11 = f32[170,128,128]{1,2,0:T(8,128)} fusion(f32[170,128,128]{2,1,0:T(8,128)} %gather_fusion.1, f32[1,1,170,128,128]{4,3,2,1,0:T(8,128)} %param.6), kind=kOutput, calls=%fused_computation.13 | convolution fusion | flops 4278190080 | bytes 33423360 | tf_op jit(solution)/shard_map/kba,kbv->kav/dot_general | solution.py:20
  168.2 12.0 %copy.14 = f32[170,128,128]{2,1,0:T(8,128)} copy(f32[170,128,128]{1,2,0:T(8,128)} %fusion.11) | data formatting | bytes 22282240 | tf_op jit(solution)/shard_map/kba,kbv->kav/dot_general | solution.py:20
  180.3 10.4 %pad.7 = f32[176,128,128]{2,1,0:T(8,128)} pad(f32[170,128,128]{2,1,0:T(8,128)} %copy.14, f32[]{:T(128)} %constant.31.clone.2), padding=0_6x0_0x0_0 | pad | bytes 22675460
  190.7 18.4 %copy.39 = f32[22,8,128,128]{3,1,2,0:T(8,128)} copy(f32[22,8,128,128]{3,2,1,0:T(8,128)} %bitcast.117) | data formatting | bytes 23068672
  209.1 7.0 fusion.33
  218.7 39.3 %reduce-scatter.7.cloned.1.call-done = f32[256,128]{1,0:T(8,128)} async-done(((f32[2048,128]{1,0:T(8,128)}), f32[256,128]{1,0:T(8,128)}) %reduce-scatter.7.cloned.1.call-update) | async-done | bytes 131088 | tf_op jit(solution)/shard_map/reduce_scatter | solution.py:56
  260.0 144.0 %all-reduce.3.cloned.1.call-done = f32[128,128]{0,1:T(8,128)} async-done(((f32[128,128]{0,1:T(8,128)}), f32[128,128]{0,1:T(8,128)}) %all-reduce.3.cloned.1.call-update) | async-done | bytes 65552 | tf_op jit(solution)/shard_map/psum | solution.py:63
  405.8 11.7 %cholesky.44 = f32[128,128]{1,0:T(8,128)S(1)} custom-call(f32[128,128]{1,0:T(8,128)S(1)} %fusion.27), custom_call_target="Cholesky" | custom-call | tf_op jit(solution)/shard_map/jit(cholesky)/cholesky | solution.py:64
  418.9 9.8 %custom-call.8 = f32[1,128,128]{1,2,0:T(8,128)S(1)} custom-call(f32[1,128,128]{2,1,0:T(8,128)S(1)} %fusion.20), custom_call_target="InvertDiagBlocksLowerTriangular" | custom-call | tf_op jit(solution)/shard_map/triangular_solve/custom-call.0 | solution.py:37
  432.6 31.0 %all-gather.7.cloned.1.call-done = f32[2048,128]{0,1:T(8,128)} async-done(((f32[256,128]{0,1:T(8,128)}), f32[2048,128]{0,1:T(8,128)}) %all-gather.7.cloned.1.call-update) | async-done | bytes 1048592 | tf_op jit(solution)/shard_map/all_gather | solution.py:52
  470.5 23.5 %fusion.14 = f32[170,128,128]{1,2,0:T(8,128)} fusion(f32[170,128,128]{2,1,0:T(8,128)} %gather_fusion.2, f32[1,1,170,128,128]{4,3,2,1,0:T(8,128)} %param.6), kind=kOutput, calls=%fused_computation.14 | convolution fusion | flops 4278190080 | bytes 33423360 | tf_op jit(solution)/shard_map/kab,kbv->kav/dot_general | solution.py:18
  494.0 12.1 %copy.20 = f32[170,128,128]{2,1,0:T(8,128)} copy(f32[170,128,128]{1,2,0:T(8,128)} %fusion.14) | data formatting | bytes 22282240 | tf_op jit(solution)/shard_map/kab,kbv->kav/dot_general | solution.py:18
  506.1 10.3 %pad.8 = f32[176,128,128]{2,1,0:T(8,128)} pad(f32[170,128,128]{2,1,0:T(8,128)} %copy.20, f32[]{:T(128)} %constant.31.clone.2), padding=0_6x0_0x0_0 | pad | bytes 22675460
  516.4 18.4 %copy.40 = f32[22,8,128,128]{3,1,2,0:T(8,128)} copy(f32[22,8,128,128]{3,2,1,0:T(8,128)} %bitcast.118) | data formatting | bytes 23068672
  534.8 7.3 fusion.30
  550.9 23.4 %fusion.17 = f32[170,128,128]{1,2,0:T(8,128)} fusion(f32[170,128,128]{2,1,0:T(8,128)} %gather_fusion.3, f32[1,1,170,128,128]{4,3,2,1,0:T(8,128)} %param.6), kind=kOutput, calls=%fused_computation.15 | convolution fusion | flops 4278190080 | bytes 33423360 | tf_op jit(solution)/shard_map/kba,kbv->kav/dot_general | solution.py:20
  574.3 12.0 %copy.23 = f32[170,128,128]{2,1,0:T(8,128)} copy(f32[170,128,128]{1,2,0:T(8,128)} %fusion.17) | data formatting | bytes 22282240 | tf_op jit(solution)/shard_map/kba,kbv->kav/dot_general | solution.py:20
  586.3 10.4 %pad.9 = f32[176,128,128]{2,1,0:T(8,128)} pad(f32[170,128,128]{2,1,0:T(8,128)} %copy.23, f32[]{:T(128)} %constant.31.clone.2), padding=0_6x0_0x0_0 | pad | bytes 22675460
  596.7 18.3 %copy.41 = f32[22,8,128,128]{3,1,2,0:T(8,128)} copy(f32[22,8,128,128]{3,2,1,0:T(8,128)} %bitcast.113) | data formatting | bytes 23068672
  615.0 6.8 fusion.32
  624.4 39.4 %reduce-scatter.11.cloned.1.call-done = f32[256,128]{1,0:T(8,128)} async-done(((f32[2048,128]{1,0:T(8,128)}), f32[256,128]{1,0:T(8,128)}) %reduce-scatter.11.cloned.1.call-update) | async-done | bytes 131088 | tf_op jit(solution)/shard_map/reduce_scatter | solution.py:56
  665.8 144.7 %all-reduce.5.cloned.1.call-done = f32[128,128]{0,1:T(8,128)} async-done(((f32[128,128]{0,1:T(8,128)}), f32[128,128]{0,1:T(8,128)}) %all-reduce.5.cloned.1.call-update) | async-done | bytes 65552 | tf_op jit(solution)/shard_map/psum | solution.py:63
  812.4 11.7 %cholesky.55 = f32[128,128]{1,0:T(8,128)S(1)} custom-call(f32[128,128]{1,0:T(8,128)S(1)} %fusion.24), custom_call_target="Cholesky" | custom-call | tf_op jit(solution)/shard_map/jit(cholesky)/cholesky | solution.py:64
  825.4 9.8 %custom-call.10 = f32[1,128,128]{1,2,0:T(8,128)S(1)} custom-call(f32[1,128,128]{2,1,0:T(8,128)S(1)} %fusion.21), custom_call_target="InvertDiagBlocksLowerTriangular" | custom-call | tf_op jit(solution)/shard_map/triangular_solve/custom-call.0 | solution.py:37
  (59 shorter events, 44.0 us)
Async XLA Ops:
  6.5 41.7 %all-gather.11.cloned.1.call-start = ((), (), s32[]{:S(2)}) async-start(), calls=%async_computation.12 | async-start | bytes 1179648 | tf_op jit(solution)/shard_map/all_gather | solution.py:52
  8.2 124.6 %all-gather.13.cloned.1.call-start = ((), (), s32[]{:S(2)}) async-start(), calls=%async_computation.13 | async-start | bytes 2228224 | tf_op jit(solution)/shard_map/all_gather | solution.py:53
  9.0 208.3 %reduce-scatter.5.cloned.1.call-start = ((), (), s32[]{:S(2)}) async-start(), calls=%async_computation.4 | async-start | bytes 2228224 | tf_op jit(solution)/shard_map/reduce_scatter | solution.py:55
  132.7 125.2 %reduce-scatter.7.cloned.1.call-start = ((), (), s32[]{:S(2)}) async-start(), calls=%async_computation.5 | async-start | bytes 1179648 | tf_op jit(solution)/shard_map/reduce_scatter | solution.py:56
  217.2 186.8 %all-reduce.3.cloned.1.call-start = ((), (), s32[]{:S(2)}) async-start(), calls=%async_computation.6 | async-start | bytes 131072 | tf_op jit(solution)/shard_map/psum | solution.py:63
  260.0 203.6 %all-gather.7.cloned.1.call-start = ((), (), s32[]{:S(2)}) async-start(), calls=%async_computation.7 | async-start | bytes 1179648 | tf_op jit(solution)/shard_map/all_gather | solution.py:52
  430.6 113.1 %all-gather.9.cloned.1.call-start = ((), (), s32[]{:S(2)}) async-start(), calls=%async_computation.9 | async-start | bytes 2228224 | tf_op jit(solution)/shard_map/all_gather | solution.py:53
  432.5 190.5 %reduce-scatter.9.cloned.1.call-start = ((), (), s32[]{:S(2)}) async-start(), calls=%async_computation.8 | async-start | bytes 2228224 | tf_op jit(solution)/shard_map/reduce_scatter | solution.py:55
  543.6 120.2 %reduce-scatter.11.cloned.1.call-start = ((), (), s32[]{:S(2)}) async-start(), calls=%async_computation.10 | async-start | bytes 1179648 | tf_op jit(solution)/shard_map/reduce_scatter | solution.py:56
  623.0 187.6 %all-reduce.5.cloned.1.call-start = ((), (), s32[]{:S(2)}) async-start(), calls=%async_computation.11 | async-start | bytes 131072 | tf_op jit(solution)/shard_map/psum | solution.py:63
Sparse Core Ops, SparseCore 0:
  9.0 39.1 all-gather.10
  50.6 52.7 all-gather.12
  132.9 73.0 reduce-scatter.4
  217.4 40.5 reduce-scatter.6
  262.5 141.4 all-reduce.2
  430.7 32.8 all-gather.6
  466.1 53.9 all-gather.8
  543.7 73.1 reduce-scatter.8
  623.1 40.6 reduce-scatter.10
  669.1 141.4 all-reduce.4
where the time goes:
time: 855 us; the launch traced here: 846 us
  waiting for transfers between devices  437 us (51%)
  local copies, waits for them, and re-layouts  210 us (25%)
  matrix products  135 us (16%)
  other arithmetic  49.9 us (6%)
  between operations  14 us (2%)
    psum x2, waiting for transfers between devices, local(): gram_sum = lax.psum(partial_gram, ('row', 'col')) / total_rows  289 us
    unnamed x8, local copies, waits for them, and re-layouts  115 us
    reduce_scatter x2, waiting for transfers between devices, local(): lax.psum_scatter(out_cols, 'row', scatter_dimension=0, tiled=True)  78.7 us
    all_gather x2, waiting for transfers between devices, local(): col_side = lax.all_gather(current[1], 'row', axis=0, tiled=True)  68.6 us
    dot_general x2, matrix products, tile_products(): jnp.einsum('kab,kbv->kav', values, col_pieces, precision=exact_mode)  46.9 us
    dot_general x2, matrix products, tile_products(): jnp.einsum('kba,kbv->kav', values, row_pieces, precision=exact_mode)  46.8 us
    another operation x6, other arithmetic, local(): factor = jnp.linalg.cholesky(gram_sum)  24.8 us
    dot_general x2, local copies, waits for them, and re-layouts, tile_products(): jnp.einsum('kab,kbv->kav', values, col_pieces, precision=exact_mode)  24.3 us
  transfers between devices with their start and end apart: 10, of which 6 were waited for; matrix products, arithmetic and copies ran while one was open for 40% of the time, Pallas kernels for 0%

commit v1 on v0

--- a/solution.py
+++ b/solution.py
@@ -60,7 +60,7 @@
         partial_gram = partial_gram + jnp.einsum(
             "nv,nw->vw", factor_lower, factor_lower, precision=exact_mode
         )
-        gram_sum = lax.psum(partial_gram, ("row", "col")) / total_rows
+        gram_sum = lax.psum(lax.psum(partial_gram, "col"), "row") / total_rows
         factor = jnp.linalg.cholesky(gram_sum)
         current = (normal_basis(applied[0], factor), normal_basis(applied[1], factor))
     upper, lower = current

time: 855 us -> 981 us (1.15)
  waiting for transfers between devices: 437 us -> 558 us
    psum x2 -> x4, waiting for transfers between devices: 289 us -> 403 us  [local(): gram_sum = lax.psum(lax.psum(partial_gram, 'col'), 'row') / total_rows]
  transfers between devices with their start and end apart: 10 -> 12, of which waited for: 6 -> 8; matrix products, arithmetic and copies ran while one was open for 40% -> 35% of each run, Pallas kernels for 0% -> 0%
where the time goes in v1:
time: 981 us; the launch traced here: 967 us
  waiting for transfers between devices  558 us (57%)
  local copies, waits for them, and re-layouts  210 us (21%)
  matrix products  135 us (14%)
  other arithmetic  49.9 us (5%)
  between operations  14 us (1%)
    psum x4, waiting for transfers between devices, local(): gram_sum = lax.psum(lax.psum(partial_gram, 'col'), 'row') / total_rows  403 us
    unnamed x8, local copies, waits for them, and re-layouts  115 us
    reduce_scatter x2, waiting for transfers between devices, local(): lax.psum_scatter(out_cols, 'row', scatter_dimension=0, tiled=True)  78.6 us
    all_gather x2, waiting for transfers between devices, local(): col_side = lax.all_gather(current[1], 'row', axis=0, tiled=True)  75.9 us
    dot_general x2, matrix products, tile_products(): jnp.einsum('kab,kbv->kav', values, col_pieces, precision=exact_mode)  46.9 us
    dot_general x2, matrix products, tile_products(): jnp.einsum('kba,kbv->kav', values, row_pieces, precision=exact_mode)  46.8 us
    another operation x6, other arithmetic, local(): factor = jnp.linalg.cholesky(gram_sum)  24.8 us
    dot_general x2, local copies, waits for them, and re-layouts, tile_products(): jnp.einsum('kab,kbv->kav', values, col_pieces, precision=exact_mode)  24.3 us
  transfers between devices with their start and end apart: 12, of which 8 were waited for; matrix products, arithmetic and copies ran while one was open for 35% of the time, Pallas kernels for 0%

profile of v1, /device:TPU:1, one launch (start us, length us, event | category | flops | bytes accessed | tf_op | source)
XLA Modules:
  0.0 967.1 jit_solution(17212985459253430292)
XLA Ops:
  10.6 37.6 %all-gather.11.cloned.1.call-done = f32[1,2048,128]{2,1,0:T(8,128)} async-done(((f32[1,256,128]{2,1,0:T(8,128)}), f32[1,2048,128]{2,1,0:T(8,128)}) %all-gather.11.cloned.1.call-update) | async-done | bytes 1048592 | tf_op jit(solution)/shard_map/all_gather | solution.py:52
  48.2 11.6 %gather_fusion = f32[170,128,128]{2,1,0:T(8,128)} fusion(f32[16,128,128]{2,1,0:T(8,128)} %bitcast.108, s32[1024]{0:T(1024)S(1)} %pad_clamp_fusion.1), kind=kCustom, calls=%fused_computation | custom fusion | bytes 22282920 | tf_op jit(solution)/shard_map/gather | solution.py:17
  59.8 23.3 %fusion.8 = f32[170,128,128]{1,2,0:T(8,128)} fusion(f32[170,128,128]{2,1,0:T(8,128)} %gather_fusion, f32[1,1,170,128,128]{4,3,2,1,0:T(8,128)} %param.6), kind=kOutput, calls=%fused_computation.12 | convolution fusion | flops 4278190080 | bytes 33423360 | tf_op jit(solution)/shard_map/kab,kbv->kav/dot_general | solution.py:18
  83.1 12.3 %copy.12 = f32[170,128,128]{2,1,0:T(8,128)} copy(f32[170,128,128]{1,2,0:T(8,128)} %fusion.8) | data formatting | bytes 22282240 | tf_op jit(solution)/shard_map/kab,kbv->kav/dot_general | solution.py:18
  95.3 10.5 %pad.6 = f32[176,128,128]{2,1,0:T(8,128)} pad(f32[170,128,128]{2,1,0:T(8,128)} %copy.12, f32[]{:T(128)} %constant.31.clone.2), padding=0_6x0_0x0_0 | pad | bytes 22675460
  105.8 18.3 %copy.38 = f32[22,8,128,128]{3,1,2,0:T(8,128)} copy(f32[22,8,128,128]{3,2,1,0:T(8,128)} %bitcast.115) | data formatting | bytes 23068672
  124.1 7.0 fusion.31
  132.8 12.0 %gather_fusion.1 = f32[170,128,128]{2,1,0:T(8,128)} fusion(f32[32,128,128]{2,1,0:T(8,128)} %bitcast.110, s32[1024]{0:T(1024)S(1)} %pad_clamp_fusion), kind=kCustom, calls=%fused_computation.1 | custom fusion | bytes 22282920 | tf_op jit(solution)/shard_map/gather | solution.py:19
  144.8 23.4 %fusion.11 = f32[170,128,128]{1,2,0:T(8,128)} fusion(f32[170,128,128]{2,1,0:T(8,128)} %gather_fusion.1, f32[1,1,170,128,128]{4,3,2,1,0:T(8,128)} %param.6), kind=kOutput, calls=%fused_computation.13 | convolution fusion | flops 4278190080 | bytes 33423360 | tf_op jit(solution)/shard_map/kba,kbv->kav/dot_general | solution.py:20
  168.2 12.0 %copy.14 = f32[170,128,128]{2,1,0:T(8,128)} copy(f32[170,128,128]{1,2,0:T(8,128)} %fusion.11) | data formatting | bytes 22282240 | tf_op jit(solution)/shard_map/kba,kbv->kav/dot_general | solution.py:20
  180.3 10.4 %pad.7 = f32[176,128,128]{2,1,0:T(8,128)} pad(f32[170,128,128]{2,1,0:T(8,128)} %copy.14, f32[]{:T(128)} %constant.31.clone.2), padding=0_6x0_0x0_0 | pad | bytes 22675460
  190.7 18.4 %copy.39 = f32[22,8,128,128]{3,1,2,0:T(8,128)} copy(f32[22,8,128,128]{3,2,1,0:T(8,128)} %bitcast.117) | data formatting | bytes 23068672
  218.7 39.3 %reduce-scatter.7.cloned.1.call-done = f32[256,128]{1,0:T(8,128)} async-done(((f32[2048,128]{1,0:T(8,128)}), f32[256,128]{1,0:T(8,128)}) %reduce-scatter.7.cloned.1.call-update) | async-done | bytes 131088 | tf_op jit(solution)/shard_map/reduce_scatter | solution.py:56
  260.0 129.8 %all-reduce.5.cloned.1.call-done = f32[128,128]{0,1:T(8,128)} async-done(((f32[128,128]{0,1:T(8,128)}), f32[128,128]{0,1:T(8,128)}) %all-reduce.5.cloned.1.call-update) | async-done | bytes 65552 | tf_op jit(solution)/shard_map/psum | solution.py:63
  389.9 71.5 %all-reduce.7.cloned.1.call-done = f32[128,128]{0,1:T(8,128)} async-done(((f32[128,128]{0,1:T(8,128)}), f32[128,128]{0,1:T(8,128)}) %all-reduce.7.cloned.1.call-update) | async-done | bytes 65552 | tf_op jit(solution)/shard_map/psum | solution.py:63
  463.2 11.7 %cholesky.44 = f32[128,128]{1,0:T(8,128)S(1)} custom-call(f32[128,128]{1,0:T(8,128)S(1)} %fusion.27), custom_call_target="Cholesky" | custom-call | tf_op jit(solution)/shard_map/jit(cholesky)/cholesky | solution.py:64
  476.2 9.8 %custom-call.8 = f32[1,128,128]{1,2,0:T(8,128)S(1)} custom-call(f32[1,128,128]{2,1,0:T(8,128)S(1)} %fusion.20), custom_call_target="InvertDiagBlocksLowerTriangular" | custom-call | tf_op jit(solution)/shard_map/triangular_solve/custom-call.0 | solution.py:37
  489.9 38.3 %all-gather.7.cloned.1.call-done = f32[2048,128]{0,1:T(8,128)} async-done(((f32[256,128]{0,1:T(8,128)}), f32[2048,128]{0,1:T(8,128)}) %all-gather.7.cloned.1.call-update) | async-done | bytes 1048592 | tf_op jit(solution)/shard_map/all_gather | solution.py:52
  535.1 23.5 %fusion.14 = f32[170,128,128]{1,2,0:T(8,128)} fusion(f32[170,128,128]{2,1,0:T(8,128)} %gather_fusion.2, f32[1,1,170,128,128]{4,3,2,1,0:T(8,128)} %param.6), kind=kOutput, calls=%fused_computation.14 | convolution fusion | flops 4278190080 | bytes 33423360 | tf_op jit(solution)/shard_map/kab,kbv->kav/dot_general | solution.py:18
  558.7 12.0 %copy.20 = f32[170,128,128]{2,1,0:T(8,128)} copy(f32[170,128,128]{1,2,0:T(8,128)} %fusion.14) | data formatting | bytes 22282240 | tf_op jit(solution)/shard_map/kab,kbv->kav/dot_general | solution.py:18
  570.7 10.3 %pad.8 = f32[176,128,128]{2,1,0:T(8,128)} pad(f32[170,128,128]{2,1,0:T(8,128)} %copy.20, f32[]{:T(128)} %constant.31.clone.2), padding=0_6x0_0x0_0 | pad | bytes 22675460
  581.1 18.4 %copy.40 = f32[22,8,128,128]{3,1,2,0:T(8,128)} copy(f32[22,8,128,128]{3,2,1,0:T(8,128)} %bitcast.118) | data formatting | bytes 23068672
  599.4 7.3 fusion.30
  615.6 23.4 %fusion.17 = f32[170,128,128]{1,2,0:T(8,128)} fusion(f32[170,128,128]{2,1,0:T(8,128)} %gather_fusion.3, f32[1,1,170,128,128]{4,3,2,1,0:T(8,128)} %param.6), kind=kOutput, calls=%fused_computation.15 | convolution fusion | flops 4278190080 | bytes 33423360 | tf_op jit(solution)/shard_map/kba,kbv->kav/dot_general | solution.py:20
  639.0 12.0 %copy.23 = f32[170,128,128]{2,1,0:T(8,128)} copy(f32[170,128,128]{1,2,0:T(8,128)} %fusion.17) | data formatting | bytes 22282240 | tf_op jit(solution)/shard_map/kba,kbv->kav/dot_general | solution.py:20
  651.0 10.4 %pad.9 = f32[176,128,128]{2,1,0:T(8,128)} pad(f32[170,128,128]{2,1,0:T(8,128)} %copy.23, f32[]{:T(128)} %constant.31.clone.2), padding=0_6x0_0x0_0 | pad | bytes 22675460
  661.4 18.3 %copy.41 = f32[22,8,128,128]{3,1,2,0:T(8,128)} copy(f32[22,8,128,128]{3,2,1,0:T(8,128)} %bitcast.113) | data formatting | bytes 23068672
  689.1 39.3 %reduce-scatter.11.cloned.1.call-done = f32[256,128]{1,0:T(8,128)} async-done(((f32[2048,128]{1,0:T(8,128)}), f32[256,128]{1,0:T(8,128)}) %reduce-scatter.11.cloned.1.call-update) | async-done | bytes 131088 | tf_op jit(solution)/shard_map/reduce_scatter | solution.py:56
  730.5 130.0 %all-reduce.9.cloned.1.call-done = f32[128,128]{0,1:T(8,128)} async-done(((f32[128,128]{0,1:T(8,128)}), f32[128,128]{0,1:T(8,128)}) %all-reduce.9.cloned.1.call-update) | async-done | bytes 65552 | tf_op jit(solution)/shard_map/psum | solution.py:63
  860.5 71.5 %all-reduce.11.cloned.1.call-done = f32[128,128]{0,1:T(8,128)} async-done(((f32[128,128]{0,1:T(8,128)}), f32[128,128]{0,1:T(8,128)}) %all-reduce.11.cloned.1.call-update) | async-done | bytes 65552 | tf_op jit(solution)/shard_map/psum | solution.py:63
  933.9 11.7 %cholesky.55 = f32[128,128]{1,0:T(8,128)S(1)} custom-call(f32[128,128]{1,0:T(8,128)S(1)} %fusion.24), custom_call_target="Cholesky" | custom-call | tf_op jit(solution)/shard_map/jit(cholesky)/cholesky | solution.py:64
  946.9 9.8 %custom-call.10 = f32[1,128,128]{1,2,0:T(8,128)S(1)} custom-call(f32[1,128,128]{2,1,0:T(8,128)S(1)} %fusion.21), custom_call_target="InvertDiagBlocksLowerTriangular" | custom-call | tf_op jit(solution)/shard_map/triangular_solve/custom-call.0 | solution.py:37
  (65 shorter events, 57.9 us)
Async XLA Ops:
  6.5 41.7 %all-gather.11.cloned.1.call-start = ((), (), s32[]{:S(2)}) async-start(), calls=%async_computation.14 | async-start | bytes 1179648 | tf_op jit(solution)/shard_map/all_gather | solution.py:52
  8.2 124.6 %all-gather.13.cloned.1.call-start = ((), (), s32[]{:S(2)}) async-start(), calls=%async_computation.15 | async-start | bytes 2228224 | tf_op jit(solution)/shard_map/all_gather | solution.py:53
  9.0 208.3 %reduce-scatter.5.cloned.1.call-start = ((), (), s32[]{:S(2)}) async-start(), calls=%async_computation.4 | async-start | bytes 2228224 | tf_op jit(solution)/shard_map/reduce_scatter | solution.py:55
  132.7 125.2 %reduce-scatter.7.cloned.1.call-start = ((), (), s32[]{:S(2)}) async-start(), calls=%async_computation.5 | async-start | bytes 1179648 | tf_op jit(solution)/shard_map/reduce_scatter | solution.py:56
  217.2 172.6 %all-reduce.5.cloned.1.call-start = ((), (), s32[]{:S(2)}) async-start(), calls=%async_computation.6 | async-start | bytes 131072 | tf_op jit(solution)/shard_map/psum | solution.py:63
  260.0 201.4 %all-reduce.7.cloned.1.call-start = ((), (), s32[]{:S(2)}) async-start(), calls=%async_computation.7 | async-start | bytes 131072 | tf_op jit(solution)/shard_map/psum | solution.py:63
  389.8 138.4 %all-gather.7.cloned.1.call-start = ((), (), s32[]{:S(2)}) async-start(), calls=%async_computation.8 | async-start | bytes 1179648 | tf_op jit(solution)/shard_map/all_gather | solution.py:52
  487.9 120.4 %all-gather.9.cloned.1.call-start = ((), (), s32[]{:S(2)}) async-start(), calls=%async_computation.10 | async-start | bytes 2228224 | tf_op jit(solution)/shard_map/all_gather | solution.py:53
  489.9 197.8 %reduce-scatter.9.cloned.1.call-start = ((), (), s32[]{:S(2)}) async-start(), calls=%async_computation.9 | async-start | bytes 2228224 | tf_op jit(solution)/shard_map/reduce_scatter | solution.py:55
  608.3 120.2 %reduce-scatter.11.cloned.1.call-start = ((), (), s32[]{:S(2)}) async-start(), calls=%async_computation.11 | async-start | bytes 1179648 | tf_op jit(solution)/shard_map/reduce_scatter | solution.py:56
  687.7 172.8 %all-reduce.9.cloned.1.call-start = ((), (), s32[]{:S(2)}) async-start(), calls=%async_computation.12 | async-start | bytes 131072 | tf_op jit(solution)/shard_map/psum | solution.py:63
  730.4 201.6 %all-reduce.11.cloned.1.call-start = ((), (), s32[]{:S(2)}) async-start(), calls=%async_computation.13 | async-start | bytes 131072 | tf_op jit(solution)/shard_map/psum | solution.py:63
Sparse Core Ops, SparseCore 0:
  9.0 39.1 all-gather.10
  50.6 52.7 all-gather.12
  132.9 73.0 reduce-scatter.4
  217.4 40.5 reduce-scatter.6
  260.3 129.4 all-reduce.4
  392.3 69.0 all-reduce.6
  488.1 40.1 all-gather.6
  530.5 53.9 all-gather.8
  608.4 73.1 reduce-scatter.8
  687.8 40.5 reduce-scatter.10
  730.9 129.5 all-reduce.8
  863.0 69.0 all-reduce.10
